TPU v7x, 256 devices: a whole 4x4x8 slice. The times are simulated.
256 devices in a mesh: lat: 8 (over z_lo, core), lon: 8 (over z_hi, x), chan: 4 (over y).
Axes of the slice: x: 4, y: 4, z: 8 (z_hi: 2, z_lo: 4; z = z_hi * 4 + z_lo), core: 2. Of those that a mesh axis runs over, the one named last changes fastest.
Arguments:
- queries: bfloat16 [128, 64, 2560], P('lat', 'lon', 'chan'), may hold values from -8 to 8
- keys: bfloat16 [128, 64, 2560], P('lat', 'lon', 'chan'), may hold values from -8 to 8
- values: bfloat16 [128, 64, 2560], P('lat', 'lon', 'chan'), may hold values from -6 to 6
- attn_out: bfloat16 [128, 64, 2560], P('lat', 'lon', 'chan'), may hold values from -6 to 6
- grad_out: bfloat16 [128, 64, 5120], P('lat', 'lon', 'chan'), may hold values from -6 to 6
- w_out: bfloat16 [5120, 2560], P(('lat', 'lon'), 'chan'), may hold values from -0.078125 to 0.078125
- bias_table: float32 [20, 25, 13], P('chan'), may hold values from -5 to 5
- key_mask: int32 [128, 64], replicated, may hold values 0 or 1
Outputs:
- grad_queries: bfloat16 [128, 64, 2560], P('lat', 'lon', 'chan')
- grad_keys: bfloat16 [128, 64, 2560], P('lat', 'lon', 'chan')
- grad_values: bfloat16 [128, 64, 2560], P('lat', 'lon', 'chan')
- grad_wout: float32 [5120, 2560], P(('lat', 'lon'), 'chan')
- grad_table: float32 [20, 25, 13], P('chan')
All inputs are finite; a program needn't handle non-finite values.
Results may differ from a plain program's by a relative error of at most 0.007.
Values may be sent and summed in bfloat16 or wider, within the bound.
No kernel may reach another device: no remote copies, remote signals or barrier semaphores. Data moves between devices by JAX's collectives and lax.ppermute only.
A program may use at most 128 MiB of HBM per device.

v0:
```python
import jax
import jax.numpy as jnp
from jax import lax
from jax.sharding import PartitionSpec as P

HEAD_DIM = 128
WIN = 13


def extended_2(value, sides, width, wrap):
    for axis, dim in sides:
        count, length = (lax.axis_size(axis), value.shape[dim])
        up = [(i, (i + 1) % count) for i in range(count if wrap else count - 1)]
        down = [(j, i) for i, j in up]
        last = lax.slice_in_dim(value, length - width, length, axis=dim)
        leading = lax.slice_in_dim(value, 0, width, axis=dim)
        before = lax.ppermute(last, axis, up)
        after = lax.ppermute(leading, axis, down)
        value = jnp.concatenate([before, value, after], axis=dim)
    return value


def fold_lon(extended, core_width):
    full_width = extended.shape[2]
    reach_cells = (full_width - core_width) // 2
    rim_cells = jnp.concatenate(
        [extended[:, :, :reach_cells], extended[:, :, full_width - reach_cells :]], axis=2
    )
    received = extended_2(rim_cells.astype(jnp.bfloat16), (("lon", 2),), reach_cells, True).astype(
        rim_cells.dtype
    )
    middle = extended[:, :, reach_cells : full_width - reach_cells]
    front_add = jnp.pad(
        received[:, :, :reach_cells], ((0, 0), (0, 0), (0, core_width - reach_cells), (0, 0))
    )
    back_add = jnp.pad(
        received[:, :, 3 * reach_cells :], ((0, 0), (0, 0), (core_width - reach_cells, 0), (0, 0))
    )
    return middle + front_add + back_add


def fold_lat(extended, core_width):
    full_width = extended.shape[1]
    reach_cells = (full_width - core_width) // 2
    rim_cells = jnp.concatenate(
        [extended[:, :reach_cells], extended[:, full_width - reach_cells :]], axis=1
    )
    received = extended_2(rim_cells.astype(jnp.bfloat16), (("lat", 1),), reach_cells, False).astype(
        rim_cells.dtype
    )
    middle = extended[:, reach_cells : full_width - reach_cells]
    front_add = jnp.pad(
        received[:, :reach_cells], ((0, 0), (0, core_width - reach_cells), (0, 0), (0, 0))
    )
    back_add = jnp.pad(
        received[:, 3 * reach_cells :], ((0, 0), (core_width - reach_cells, 0), (0, 0), (0, 0))
    )
    return middle + front_add + back_add


def local(queries, keys, values, attn_out, grad_out, w_out, bias_table, key_mask):
    lat_rows, lon_cols, chan_width = queries.shape
    head_count = bias_table.shape[0]
    reach_cells = WIN // 2
    score_scale = HEAD_DIM ** (-0.5)
    tokens = lat_rows * lon_cols
    ext_rows = lat_rows + 2 * reach_cells
    ext_cols = lon_cols + 2 * reach_cells
    row_block = 4
    key_span = row_block + WIN - 1
    block_count = lat_rows // row_block
    block_rows = row_block * lon_cols
    block_keys = key_span * ext_cols
    offset_rows = 2 * WIN - 1
    low_pad = row_block - 1
    lat_total = lat_rows * lax.axis_size("lat")
    lon_total = lon_cols * lax.axis_size("lon")
    contract_lead = (((0,), (0,)), ((), ()))
    full_grad = lax.all_gather(grad_out, "chan", axis=2, tiled=True).reshape(tokens, -1)
    grad_cols = jnp.transpose(full_grad)
    slab_part = grad_cols
    grad_attn = lax.dot_general(
        slab_part,
        lax.all_gather(w_out, ("lat", "lon"), axis=0, tiled=True),
        contract_lead,
        preferred_element_type=jnp.float32,
    ).astype(jnp.bfloat16)
    kv_pair = jnp.stack([keys, values])
    extended = extended_2(kv_pair, (("lat", 1), ("lon", 2)), reach_cells, True)
    lat_first = lax.axis_index("lat") * lat_rows
    lon_first = lax.axis_index("lon") * lon_cols
    ext_col = lon_first - reach_cells + jnp.arange(ext_cols, dtype=jnp.int32)
    wrap_col = ext_col % lon_total
    mask_cols = jnp.take(key_mask, wrap_col, axis=1)
    mark_cols = wrap_col % 4 == 0
    rel_lon = (
        jnp.arange(ext_cols, dtype=jnp.int32)[None, :]
        - jnp.arange(lon_cols, dtype=jnp.int32)[:, None]
    )
    in_lon = (rel_lon >= 0) & (rel_lon < WIN)
    lon_pick = jnp.clip(rel_lon, 0, WIN - 1)
    lon_table = jnp.take(bias_table, lon_pick, axis=2).transpose(0, 2, 1, 3)
    table_pad = jnp.pad(lon_table, ((0, 0), (0, 0), (low_pad, low_pad), (0, 0)))
    query_heads = queries.reshape(lat_rows, lon_cols, head_count, HEAD_DIM)
    grad_heads = grad_attn.reshape(lat_rows, lon_cols, head_count, HEAD_DIM)

    def block_step(state_pair, block_index):
        grad_pair, table_acc = state_pair
        local_first = block_index * row_block
        top_row = lat_first + local_first
        key_first = jnp.clip(top_row - reach_cells, 0, lat_total - key_span)
        key_local = key_first - (lat_first - reach_cells)
        query_rows = top_row + jnp.arange(row_block, dtype=jnp.int32)
        window_first = jnp.clip(query_rows - reach_cells, 0, lat_total - WIN)
        key_glob = key_first + jnp.arange(key_span, dtype=jnp.int32)
        in_lat = (key_glob[None, :] >= window_first[:, None]) & (
            key_glob[None, :] < window_first[:, None] + WIN
        )
        mask_rows = lax.dynamic_slice_in_dim(mask_cols, key_first, key_span, 0)
        valid_keys = (mask_rows == 1) | (key_glob % 4 == 0)[:, None] & mark_cols[None, :]
        allowed = in_lat[:, None, :, None] & in_lon[None, :, None, :] & valid_keys[None, None, :, :]
        allowed = allowed.reshape(block_rows, block_keys)
        shifts = key_first - query_rows + (WIN - 1) + low_pad
        bias_parts = [
            lax.dynamic_slice_in_dim(table_pad, shifts[row_pos], key_span, 2)
            for row_pos in range(row_block)
        ]
        bias_rows = jnp.stack(bias_parts, axis=1).reshape(head_count, block_rows, block_keys)
        query_block = lax.dynamic_slice_in_dim(query_heads, local_first, row_block, 0).reshape(
            block_rows, head_count, HEAD_DIM
        )
        grad_block = lax.dynamic_slice_in_dim(grad_heads, local_first, row_block, 0).reshape(
            block_rows, head_count, HEAD_DIM
        )
        pair_block = lax.dynamic_slice_in_dim(extended, key_local, key_span, 1).reshape(
            2, block_keys, head_count, HEAD_DIM
        )
        key_block = pair_block[0]
        value_block = pair_block[1]
        scores = (
            score_scale
            * jnp.einsum("qhd,khd->hqk", query_block, key_block, preferred_element_type=jnp.float32)
            + bias_rows
        )
        scores = jnp.where(allowed[None], scores, -1e30)
        row_max = jnp.max(scores, axis=2, keepdims=True)
        weights_exp = jnp.exp(scores - row_max)
        prob_rows = weights_exp / jnp.sum(weights_exp, axis=2, keepdims=True)
        grad_prob = jnp.einsum(
            "qhd,khd->hqk", grad_block, value_block, preferred_element_type=jnp.float32
        )
        row_delta = jnp.sum(prob_rows * grad_prob, axis=2, keepdims=True)
        dscore = prob_rows * (grad_prob - row_delta)
        score_grid = dscore.reshape(head_count, row_block, lon_cols, key_span, ext_cols)
        score_grid = score_grid.transpose(0, 1, 3, 2, 4).reshape(
            head_count, row_block, key_span, lon_cols * ext_cols
        )
        for row_pos in range(row_block):
            prior_sum = lax.dynamic_slice_in_dim(table_acc, shifts[row_pos], key_span, 1)
            table_acc = lax.dynamic_update_slice_in_dim(
                table_acc, prior_sum + score_grid[:, row_pos], shifts[row_pos], 1
            )
        dscore_low = dscore.astype(jnp.bfloat16)
        prob_low = prob_rows.astype(jnp.bfloat16)
        grad_query = (
            score_scale
            * jnp.einsum("hqk,khd->qhd", dscore_low, key_block, preferred_element_type=jnp.float32)
        ).astype(jnp.bfloat16)
        key_part = score_scale * jnp.einsum(
            "hqk,qhd->khd", dscore_low, query_block, preferred_element_type=jnp.float32
        )
        value_part = jnp.einsum(
            "hqk,qhd->khd", prob_low, grad_block, preferred_element_type=jnp.float32
        )
        new_part = jnp.stack([key_part, value_part]).reshape(2, key_span, ext_cols, chan_width)
        prior_pair = lax.dynamic_slice_in_dim(grad_pair, key_local, key_span, 1)
        grad_pair = lax.dynamic_update_slice_in_dim(grad_pair, prior_pair + new_part, key_local, 1)
        return ((grad_pair, table_acc), grad_query)

    zero_pair = jnp.zeros((2, ext_rows, ext_cols, chan_width), jnp.float32)
    zero_table = jnp.zeros(
        (head_count, offset_rows + 2 * low_pad, lon_cols * ext_cols), jnp.float32
    )
    (grad_pair, table_acc), query_blocks = lax.scan(
        block_step, (zero_pair, zero_table), jnp.arange(block_count, dtype=jnp.int32)
    )
    grad_queries = query_blocks.reshape(lat_rows, lon_cols, chan_width)
    table_core = table_acc[:, low_pad : low_pad + offset_rows].reshape(
        head_count, offset_rows, lon_cols, ext_cols
    )
    col_take = (
        jnp.arange(lon_cols, dtype=jnp.int32)[:, None] + jnp.arange(WIN, dtype=jnp.int32)[None, :]
    )
    col_take = jnp.broadcast_to(
        col_take[None, None, :, :], (head_count, offset_rows, lon_cols, WIN)
    )
    table_local = jnp.sum(jnp.take_along_axis(table_core, col_take, axis=3), axis=2)
    grad_table = lax.psum(table_local, ("lat", "lon"))
    folded = fold_lat(fold_lon(grad_pair, lon_cols), lat_rows)
    grad_keys = folded[0].astype(jnp.bfloat16)
    grad_values = folded[1].astype(jnp.bfloat16)
    saved_out = attn_out.reshape(tokens, chan_width)
    slab_part = grad_cols
    grad_wout = lax.psum_scatter(
        jnp.dot(slab_part, saved_out, preferred_element_type=jnp.float32),
        ("lat", "lon"),
        scatter_dimension=0,
        tiled=True,
    )
    return (grad_queries, grad_keys, grad_values, grad_wout, grad_table)


def solution(mesh):
    return jax.shard_map(
        local,
        mesh=mesh,
        in_specs=(
            P("lat", "lon", "chan"),
            P("lat", "lon", "chan"),
            P("lat", "lon", "chan"),
            P("lat", "lon", "chan"),
            P("lat", "lon", "chan"),
            P(("lat", "lon"), "chan"),
            P("chan", None, None),
            P(),
        ),
        out_specs=(
            P("lat", "lon", "chan"),
            P("lat", "lon", "chan"),
            P("lat", "lon", "chan"),
            P(("lat", "lon"), "chan"),
            P("chan", None, None),
        ),
        check_vma=False,
    )
```

profile of v0, /device:TPU:240, one launch (start us, length us, event | category | flops | bytes accessed | tf_op | source)
XLA Modules:
  0.0 933.4 jit_solution(14924076082434811027)
XLA Ops:
  7.2 1.8 copy.63
  9.8 26.9 %all-gather.3.cloned.1.call-done = bf16[16,8,5120]{2,0,1:T(8,128)(2,1)} async-done(((bf16[16,8,1280]{2,0,1:T(8,128)(2,1)}), bf16[16,8,5120]{2,0,1:T(8,128)(2,1)}) %all-gather.3.cloned.1.call-update) | async-done | bytes 1310736 | tf_op jit(solution)/shard_map/all_gather | solution.py:79
  36.7 7.9 convolution_bitcast_fusion.1
  44.7 0.9 copy-done.9
  45.8 1.7 collective-permute-start.1
  49.0 1.0 collective-permute-done
  51.5 4.6 collective-permute-start.3
  56.1 1.4 gather_fusion.1
  58.2 0.9 pad.20.clone
  59.1 11.4 %collective-permute-done.3 = bf16[2,28,6,640]{3,0,2,1:T(2,128)(2,1)S(1)} collective-permute-done((bf16[2,28,6,640]{3,0,2,1:T(2,128)(2,1)S(1)}, bf16[2,28,6,640]{3,0,2,1:T(2,128)(2,1)S(1)}, u32[]{:S(2)}, u32[]{:S(2)}) %collective-permute-start.3) | collective-permute-done | bytes 430112 | tf_op jit(solution)/shard_map/ppermute | solution.py:18
  70.6 10.3 %collective-permute-done.2 = bf16[2,28,6,640]{3,0,2,1:T(2,128)(2,1)S(1)} collective-permute-done((bf16[2,28,6,640]{3,0,2,1:T(2,128)(2,1)S(1)}, bf16[2,28,6,640]{3,0,2,1:T(2,128)(2,1)S(1)}, u32[]{:S(2)}, u32[]{:S(2)}) %collective-permute-start.2) | collective-permute-done | bytes 430112 | tf_op jit(solution)/shard_map/ppermute | solution.py:17
  80.9 2.1 pad_maximum_fusion.1
  83.0 156.4 %all-gather.5.cloned.1.call-done = bf16[5120,640]{1,0:T(8,128)(2,1)} async-done(((bf16[80,640]{1,0:T(8,128)(2,1)}), bf16[5120,640]{1,0:T(8,128)(2,1)}) %all-gather.5.cloned.1.call-update) | async-done | bytes 6553616 | tf_op jit(solution)/shard_map/all_gather | solution.py:84
  239.4 4.6 fusion.42
  244.0 1.9 broadcast_in_dim.94
  245.9 117.0 %while.18 = (s32[]{:T(128)}, f32[2,28,20,640]{3,2,1,0:T(8,128)}, f32[5,31,160]{2,1,0:T(8,128)S(1)}, bf16[4,32,5,128]{3,1,2,0:T(8,128)(2,1)}, s32[4]{0:T(128)S(1)...) while((s32[]{:T(128)}, f32[2,28,20,640]{3,2,1,0:T(8,128)}, ...), condition=%wide.region_4.5_spmd.clone, body=%wide.region_0.0_spmd.clone.sunk | while | flops 67648624 | bytes 32509632 | solution.py:184
  247.3 0.8 fusion.102
  257.6 1.3 constant_dynamic-slice_fusion.7
  259.8 1.9 dynamic-slice_bitcast_fusion.5
  262.7 0.9 fusion.104
  264.0 0.8 fusion.111
  265.9 1.2 stack.66
  268.0 1.2 stack.67
  269.2 0.8 reshape.367
  272.1 3.0 fusion.106
  286.0 0.8 constant_dynamic-slice_fusion.6
  286.8 1.3 constant_dynamic-slice_fusion.7
  289.0 1.9 dynamic-slice_bitcast_fusion.5
  291.9 0.9 fusion.104
  293.3 0.8 fusion.111
  295.2 1.2 stack.66
  297.2 1.2 stack.67
  298.4 0.8 reshape.367
  301.4 3.0 fusion.106
  305.8 0.8 fusion.102
  316.0 1.3 constant_dynamic-slice_fusion.7
  318.3 1.9 dynamic-slice_bitcast_fusion.5
  321.1 0.9 fusion.104
  322.5 0.8 fusion.111
  324.4 1.2 stack.66
  326.4 1.2 stack.67
  327.6 0.8 reshape.367
  330.6 3.1 fusion.106
  335.0 0.8 fusion.102
  345.3 1.3 constant_dynamic-slice_fusion.7
  347.5 1.9 dynamic-slice_bitcast_fusion.5
  350.4 0.9 fusion.104
  351.8 0.8 fusion.111
  353.6 1.2 stack.66
  355.7 1.2 stack.67
  356.9 0.8 reshape.367
  359.8 3.1 fusion.106
  363.0 2.2 convert.16
  365.3 1.1 copy.70
  366.5 1.1 copy.71
  367.6 2.0 collective-permute-start.4
  370.2 0.9 reshape.332
  371.3 155.3 %gather_fusion.2 = f32[13000]{0:T(1024)S(1)} fusion(f32[5,25,8,20]{3,2,1,0:T(8,128)S(1)} %reshape.333, s32[13000]{0:T(1024)S(1)} %reshape.350), kind=kCustom, calls=%fused_computation.2 | custom fusion | bytes 312000 | tf_op jit(solution)/shard_map/jit(take_along_axis)/gather | solution.py:197
  527.0 1.1 copy.73
  528.1 1.1 copy.72
  529.9 2.3 fusion.59
  532.3 2.1 collective-permute-start.6
  534.3 4.4 collective-permute-start.7
  539.0 386.1 %psum.7 = f32[5,25,13]{2,1,0:T(8,128)S(1)} all-reduce(f32[5,25,13]{2,1,0:T(8,128)S(1)} %select_reduce_fusion), channel_id=1, replica_groups=mesh['lat'=8,'lon'=8,'chan'=4] {'lat','lon'}, use_global_device_ids=true, to_apply=%region_7.8 | all-reduce | flops 1625 | bytes 13000 | tf_op jit(solution)/shard_map/psum | solution.py:198
  (265 shorter events, 44.5 us)
Async XLA Ops:
  7.2 29.5 %copy-start = (bf16[16,8,640]{2,1,0:T(8,128)(2,1)S(1)}, bf16[16,8,640]{2,1,0:T(8,128)(2,1)}, u32[]{:S(2)}) copy-start(bf16[16,8,640]{2,1,0:T(8,128)(2,1)} %param.13) | copy-start | bytes 491524
  7.2 29.5 %all-gather.3.cloned.1.call-start = ((), (), s32[]{:S(2)}) async-start(), calls=%async_computation.1 | async-start | bytes 1638400 | tf_op jit(solution)/shard_map/all_gather | solution.py:79
  9.0 230.4 %all-gather.5.cloned.1.call-start = ((), (), s32[]{:S(2)}) async-start(), calls=%async_computation.2 | async-start | bytes 6656000 | tf_op jit(solution)/shard_map/all_gather | solution.py:84
  9.8 917.1 %reduce-scatter.2.cloned.1.call-start = ((), (), s32[]{:S(2)}) async-start(), calls=%async_computation.3 | async-start | bytes 13312000 | tf_op jit(solution)/shard_map/reduce_scatter | solution.py:204
  44.6 0.9 copy-start.9
  44.6 1.0 copy-start.10
  44.6 3.0 copy-start.8
  45.7 4.4 collective-permute-start
  45.8 4.8 collective-permute-start.1
  50.6 5.5 copy-start.1
  51.5 19.0 %collective-permute-start.3 = (bf16[2,28,6,640]{3,0,2,1:T(2,128)(2,1)S(1)}, bf16[2,28,6,640]{3,0,2,1:T(2,128)(2,1)S(1)}, u32[]{:S(2)}, u32[]{:S(2)}) collective-permute-start(bf16[2,28,6,640]{3,0,2,1:T(2,128)(2,1)S(1)} %copy.59), channel_id=1, source_target_pairs={{4,0},{8,4},{12,8},{16,12},{20,16},{24,20},{28,24},{0,28},{5,1},{9... | collective-permute-start | bytes 1290248 | tf_op jit(solution)/shard_map/ppermute | solution.py:18
  56.1 24.7 %collective-permute-start.2 = (bf16[2,28,6,640]{3,0,2,1:T(2,128)(2,1)S(1)}, bf16[2,28,6,640]{3,0,2,1:T(2,128)(2,1)S(1)}, u32[]{:S(2)}, u32[]{:S(2)}) collective-permute-start(bf16[2,28,6,640]{3,0,2,1:T(2,128)(2,1)S(1)} %copy.58), channel_id=1, source_target_pairs={{0,4},{4,8},{8,12},{12,16},{16,20},{20,24},{24,28},{28,0},{1,5},{5... | collective-permute-start | bytes 1290248 | tf_op jit(solution)/shard_map/ppermute | solution.py:17
  80.9 158.5 %copy-start.11 = (bf16[16,8,5120]{2,0,1:T(8,128)(2,1)S(1)}, bf16[16,8,5120]{2,0,1:T(8,128)(2,1)}, u32[]{:S(2)}) copy-start(bf16[16,8,5120]{2,0,1:T(8,128)(2,1)} %all-gather.3.cloned.1.call-done) | copy-start | bytes 3932164
  245.9 13.4 %copy-start.12 = (bf16[16,8,5,128]{3,1,2,0:T(8,128)(2,1)}, bf16[16,8,5,128]{3,1,2,0:T(8,128)(2,1)S(1)}, u32[]{:S(2)}) copy-start(bf16[16,8,5,128]{3,1,2,0:T(8,128)(2,1)S(1)} %get-tuple-element.541) | copy-start | bytes 491524 | tf_op jit(solution)/shard_map/while
  270.5 1.5 copy-start.2
  270.9 1.3 copy-start.3
  272.1 3.0 copy-start.13
  275.2 13.4 %copy-start.12 = (bf16[16,8,5,128]{3,1,2,0:T(8,128)(2,1)}, bf16[16,8,5,128]{3,1,2,0:T(8,128)(2,1)S(1)}, u32[]{:S(2)}) copy-start(bf16[16,8,5,128]{3,1,2,0:T(8,128)(2,1)S(1)} %get-tuple-element.541) | copy-start | bytes 491524 | tf_op jit(solution)/shard_map/while
  299.7 1.5 copy-start.2
  300.1 1.3 copy-start.3
  301.4 3.0 copy-start.13
  304.4 13.4 %copy-start.12 = (bf16[16,8,5,128]{3,1,2,0:T(8,128)(2,1)}, bf16[16,8,5,128]{3,1,2,0:T(8,128)(2,1)S(1)}, u32[]{:S(2)}) copy-start(bf16[16,8,5,128]{3,1,2,0:T(8,128)(2,1)S(1)} %get-tuple-element.541) | copy-start | bytes 491524 | tf_op jit(solution)/shard_map/while
  328.9 1.5 copy-start.2
  329.3 1.3 copy-start.3
  330.6 3.1 copy-start.13
  333.6 13.4 %copy-start.12 = (bf16[16,8,5,128]{3,1,2,0:T(8,128)(2,1)}, bf16[16,8,5,128]{3,1,2,0:T(8,128)(2,1)S(1)}, u32[]{:S(2)}) copy-start(bf16[16,8,5,128]{3,1,2,0:T(8,128)(2,1)S(1)} %get-tuple-element.541) | copy-start | bytes 491524 | tf_op jit(solution)/shard_map/while
  358.2 1.5 copy-start.2
  358.6 1.3 copy-start.3
  359.8 3.1 copy-start.13
  365.3 4.3 copy-start.4
  365.3 4.3 copy-start.6
  365.3 4.7 copy-start.14
  367.6 159.4 %collective-permute-start.5 = (bf16[2,28,6,640]{3,0,2,1:T(2,128)(2,1)}, bf16[2,28,6,640]{3,0,2,1:T(2,128)(2,1)}, u32[]{:S(2)}, u32[]{:S(2)}) collective-permute-start(bf16[2,28,6,640]{3,0,2,1:T(2,128)(2,1)} %copy.71), channel_id=1, source_target_pairs={{4,0},{8,4},{12,8},{16,12},{20,16},{24,20},{28,24},{0,28},{5,1},{9... | collective-permute-start | bytes 1290248 | tf_op jit(solution)/shard_map/ppermute | solution.py:18
  367.6 160.5 %collective-permute-start.4 = (bf16[2,28,6,640]{3,0,2,1:T(2,128)(2,1)}, bf16[2,28,6,640]{3,0,2,1:T(2,128)(2,1)}, u32[]{:S(2)}, u32[]{:S(2)}) collective-permute-start(bf16[2,28,6,640]{3,0,2,1:T(2,128)(2,1)} %copy.70), channel_id=1, source_target_pairs={{0,4},{4,8},{8,12},{12,16},{16,20},{20,24},{24,28},{28,0},{1,5},{5... | collective-permute-start | bytes 1290248 | tf_op jit(solution)/shard_map/ppermute | solution.py:17
  369.6 1.7 copy-start.19
  369.6 1.7 copy-start.15
  369.6 1.7 copy-start.17
  526.6 2.6 copy-start.5
  526.6 2.6 copy-start.7
  529.2 0.7 copy-start.21
  529.9 8.9 copy-start.16
  529.9 8.9 copy-start.18
  529.9 8.9 copy-start.20
  532.2 393.8 %copy-start.22 = (pred[16]{0:T(512)(128)(4,1)S(1)}, pred[16]{0:T(512)(128)(4,1)}, u32[]{:S(2)}) copy-start(pred[16]{0:T(512)(128)(4,1)} %constant.227.clone.1) | copy-start | bytes 52
  532.3 393.6 %collective-permute-start.6 = (bf16[2,6,8,640]{3,2,1,0:T(8,128)(2,1)S(1)}, bf16[2,6,8,640]{3,2,1,0:T(8,128)(2,1)S(1)}, u32[]{:S(2)}, u32[]{:S(2)}) collective-permute-start(bf16[2,6,8,640]{3,2,1,0:T(8,128)(2,1)S(1)} %get-tuple-element.361), channel_id=1, source_target_pairs={{0,32},{32,64},{64,96},{96,128},{128,160},{160,192},{192,224},{1,3... | collective-permute-start | bytes 368648 | tf_op jit(solution)/shard_map/ppermute | solution.py:17
  534.3 391.5 %collective-permute-start.7 = (bf16[2,6,8,640]{3,2,1,0:T(8,128)(2,1)S(1)}, bf16[2,6,8,640]{3,2,1,0:T(8,128)(2,1)S(1)}, u32[]{:S(2)}, u32[]{:S(2)}) collective-permute-start(bf16[2,6,8,640]{3,2,1,0:T(8,128)(2,1)S(1)} %get-tuple-element.362), channel_id=1, source_target_pairs={{32,0},{64,32},{96,64},{128,96},{160,128},{192,160},{224,192},{33,... | collective-permute-start | bytes 368648 | tf_op jit(solution)/shard_map/ppermute | solution.py:18
Sparse Core Ops, SparseCore 0:
  9.8 26.8 all-gather.2
  38.5 200.8 all-gather.4
  242.6 461.3 reduce-scatter.1
where the time goes:
time: 935 us; the launch traced here: 933 us
  blocking collectives  386 us (41%)
  local copies, waits for them, and re-layouts  227 us (24%)
  waiting for transfers between devices  207 us (22%)
  loops' own time  33.7 us (4%)
  other arithmetic  28.7 us (3%)
  matrix products  21.7 us (2%)
  starting transfers between devices  15.1 us (2%)
  between operations  14.2 us (2%)
    psum x1, blocking collectives, local(): grad_table = lax.psum(table_local, ('lat', 'lon'))  386 us
    all_gather x1, waiting for transfers between devices, local(): lax.all_gather(w_out, ('lat', 'lon'), axis=0, tiled=True)  156 us
    gather x3, local copies, waits for them, and re-layouts, local(): jnp.take_along_axis(table_core, col_take, axis=3)  156 us
    another operation x1, loops' own time, local(): lax.scan(block_step, (zero_pair, zero_table), jnp.arange(block_count, dty...  33.7 us
    all_gather x1, waiting for transfers between devices, local(): lax.all_gather(grad_out, 'chan', axis=2, tiled=True).reshape(tokens, -1)  26.9 us
  transfers between devices with their start and end apart: 11, of which 6 were waited for; matrix products, arithmetic and copies ran while one was open for 29% of the time, Pallas kernels for 0%

commit v1 on v0

--- a/solution.py
+++ b/solution.py
@@ -195,7 +195,7 @@
         col_take[None, None, :, :], (head_count, offset_rows, lon_cols, WIN)
     )
     table_local = jnp.sum(jnp.take_along_axis(table_core, col_take, axis=3), axis=2)
-    grad_table = lax.psum(table_local, ("lat", "lon"))
+    grad_table = lax.psum(lax.psum(table_local, "lat"), "lon")
     folded = fold_lat(fold_lon(grad_pair, lon_cols), lat_rows)
     grad_keys = folded[0].astype(jnp.bfloat16)
     grad_values = folded[1].astype(jnp.bfloat16)

time: 935 us -> 720 us (0.77)
  blocking collectives: 386 us -> 91 us
  waiting for transfers between devices: 207 us -> 288 us
    psum x1 -> x2, blocking collectives: 386 us -> 91 us  [local(): grad_table = lax.psum(lax.psum(table_local, 'lat'), 'lon')]
    reduce_scatter x1, waiting for transfers between devices: 0.01 us -> 79.7 us  [local(): lax.psum_scatter(jnp.dot(slab_part, saved_out, preferred_element_type=jnp...]
  transfers between devices with their start and end apart: 11 -> 11, of which waited for: 6 -> 7; matrix products, arithmetic and copies ran while one was open for 29% -> 38% of each run, Pallas kernels for 0% -> 0%
where the time goes in v1:
time: 720 us; the launch traced here: 718 us
  waiting for transfers between devices  288 us (40%)
  local copies, waits for them, and re-layouts  227 us (32%)
  blocking collectives  91 us (13%)
  loops' own time  33.9 us (5%)
  other arithmetic  28.8 us (4%)
  matrix products  21.7 us (3%)
  starting transfers between devices  14.2 us (2%)
  between operations  14.2 us (2%)
    all_gather x1, waiting for transfers between devices, local(): lax.all_gather(w_out, ('lat', 'lon'), axis=0, tiled=True)  157 us
    gather x3, local copies, waits for them, and re-layouts, local(): jnp.take_along_axis(table_core, col_take, axis=3)  156 us
    psum x2, blocking collectives, local(): grad_table = lax.psum(lax.psum(table_local, 'lat'), 'lon')  91 us
    reduce_scatter x1, waiting for transfers between devices, local(): lax.psum_scatter(jnp.dot(slab_part, saved_out, preferred_element_type=jnp...  79.7 us
    another operation x1, loops' own time, local(): lax.scan(block_step, (zero_pair, zero_table), jnp.arange(block_count, dty...  33.9 us
    all_gather x1, waiting for transfers between devices, local(): lax.all_gather(grad_out, 'chan', axis=2, tiled=True).reshape(tokens, -1)  26.9 us
  transfers between devices with their start and end apart: 11, of which 7 were waited for; matrix products, arithmetic and copies ran while one was open for 38% of the time, Pallas kernels for 0%

profile of v1, /device:TPU:240, one launch (start us, length us, event | category | flops | bytes accessed | tf_op | source)
XLA Modules:
  0.0 718.4 jit_solution(3827037467602790548)
XLA Ops:
  7.2 1.8 copy.63
  9.8 26.9 %all-gather.3.cloned.1.call-done = bf16[16,8,5120]{2,0,1:T(8,128)(2,1)} async-done(((bf16[16,8,1280]{2,0,1:T(8,128)(2,1)}), bf16[16,8,5120]{2,0,1:T(8,128)(2,1)}) %all-gather.3.cloned.1.call-update) | async-done | bytes 1310736 | tf_op jit(solution)/shard_map/all_gather | solution.py:79
  36.7 7.9 %convolution_bitcast_fusion.1 = f32[5120,640]{1,0:T(8,128)} fusion(bf16[16,8,5120]{2,0,1:T(8,128)(2,1)} %all-gather.3.cloned.1.call-done, bf16[16,8,640]{2,1,0:T(8,128)(2,1)S(1)} %copy-done), kind=kOutput, calls=%fused_computation.77 | convolution fusion | flops 838860800 | bytes 14581760 | tf_op jit(solution)/shard_map/dot_general | solution.py:205
  44.7 0.9 copy-done.9
  45.8 1.7 collective-permute-start.1
  49.0 1.0 collective-permute-done
  51.5 4.6 collective-permute-start.3
  56.2 1.4 gather_fusion.1
  58.2 0.9 pad.20.clone
  59.1 11.3 %collective-permute-done.3 = bf16[2,28,6,640]{3,0,2,1:T(2,128)(2,1)S(1)} collective-permute-done((bf16[2,28,6,640]{3,0,2,1:T(2,128)(2,1)S(1)}, bf16[2,28,6,640]{3,0,2,1:T(2,128)(2,1)S(1)}, u32[]{:S(2)}, u32[]{:S(2)}) %collective-permute-start.3) | collective-permute-done | bytes 430112 | tf_op jit(solution)/shard_map/ppermute | solution.py:18
  70.5 10.5 %collective-permute-done.2 = bf16[2,28,6,640]{3,0,2,1:T(2,128)(2,1)S(1)} collective-permute-done((bf16[2,28,6,640]{3,0,2,1:T(2,128)(2,1)S(1)}, bf16[2,28,6,640]{3,0,2,1:T(2,128)(2,1)S(1)}, u32[]{:S(2)}, u32[]{:S(2)}) %collective-permute-start.2) | collective-permute-done | bytes 430112 | tf_op jit(solution)/shard_map/ppermute | solution.py:17
  81.0 2.1 pad_maximum_fusion.1
  83.1 157.3 %all-gather.5.cloned.1.call-done = bf16[5120,640]{1,0:T(8,128)(2,1)} async-done(((bf16[80,640]{1,0:T(8,128)(2,1)}), bf16[5120,640]{1,0:T(8,128)(2,1)}) %all-gather.5.cloned.1.call-update) | async-done | bytes 6553616 | tf_op jit(solution)/shard_map/all_gather | solution.py:84
  240.4 4.6 fusion.42
  245.0 1.9 broadcast_in_dim.94
  246.9 117.3 %while.18 = (s32[]{:T(128)}, f32[2,28,20,640]{3,2,1,0:T(8,128)}, f32[5,31,160]{2,1,0:T(8,128)S(1)}, bf16[4,32,5,128]{3,1,2,0:T(8,128)(2,1)}, s32[4]{0:T(128)S(1)...) while((s32[]{:T(128)}, f32[2,28,20,640]{3,2,1,0:T(8,128)}, ...), condition=%wide.region_4.5_spmd.clone, body=%wide.region_0.0_spmd.clone.sunk | while | flops 67648624 | bytes 32509632 | solution.py:184
  248.2 0.8 fusion.102
  258.6 1.3 constant_dynamic-slice_fusion.7
  260.8 1.9 dynamic-slice_bitcast_fusion.5
  263.7 0.9 fusion.104
  265.1 0.8 fusion.111
  266.9 1.2 stack.66
  269.0 1.2 stack.67
  270.2 0.8 reshape.367
  273.2 3.1 fusion.106
  287.9 1.3 constant_dynamic-slice_fusion.7
  290.1 1.9 dynamic-slice_bitcast_fusion.5
  293.0 0.9 fusion.104
  294.4 0.8 fusion.111
  296.2 1.2 stack.66
  298.3 1.2 stack.67
  299.5 0.8 reshape.367
  302.5 3.1 fusion.106
  306.8 0.8 fusion.102
  317.2 1.3 constant_dynamic-slice_fusion.7
  319.4 1.9 dynamic-slice_bitcast_fusion.5
  322.3 0.9 fusion.104
  323.6 0.8 fusion.111
  325.5 1.2 stack.66
  327.6 1.2 stack.67
  328.8 0.8 reshape.367
  331.7 3.1 fusion.106
  346.5 1.3 constant_dynamic-slice_fusion.7
  348.7 1.9 dynamic-slice_bitcast_fusion.5
  351.6 0.9 fusion.104
  353.0 0.8 fusion.111
  354.9 1.2 stack.66
  356.9 1.2 stack.67
  358.1 0.8 reshape.367
  361.1 3.1 fusion.106
  364.2 2.2 convert.16
  366.6 1.1 copy.70
  367.7 1.1 copy.71
  368.8 2.0 collective-permute-start.4
  371.4 0.9 reshape.332
  372.5 155.3 %gather_fusion.2 = f32[13000]{0:T(1024)S(1)} fusion(f32[5,25,8,20]{3,2,1,0:T(8,128)S(1)} %reshape.333, s32[13000]{0:T(1024)S(1)} %reshape.350), kind=kCustom, calls=%fused_computation.2 | custom fusion | bytes 312000 | tf_op jit(solution)/shard_map/jit(take_along_axis)/gather | solution.py:197
  528.2 1.1 copy.73
  529.3 1.1 copy.72
  531.1 2.4 fusion.59
  533.5 1.9 collective-permute-start.6
  535.4 3.7 collective-permute-start.7
  539.3 34.0 %psum.14 = f32[5,25,13]{2,1,0:T(8,128)S(1)} all-reduce(f32[5,25,13]{2,1,0:T(8,128)S(1)} %select_reduce_fusion), channel_id=1, replica_groups=mesh['lat'=8,'lon'=8,'chan'=4] {'lat'}, use_global_device_ids=true, to_apply=%region_7.8 | all-reduce | flops 1625 | bytes 13000 | tf_op jit(solution)/shard_map/psum | solution.py:198
  573.3 57.0 %psum.15 = f32[5,25,13]{2,1,0:T(8,128)S(1)} all-reduce(f32[5,25,13]{2,1,0:T(8,128)S(1)} %psum.14), channel_id=1, replica_groups=mesh['lat'=8,'lon'=8,'chan'=4] {'lon'}, use_global_device_ids=true, to_apply=%region_8.9 | all-reduce | flops 1625 | bytes 13000 | tf_op jit(solution)/shard_map/psum | solution.py:198
  632.1 79.7 %reduce-scatter.2.cloned.1.call-done = f32[80,640]{1,0:T(8,128)} async-done(((f32[5120,640]{1,0:T(8,128)}), f32[80,640]{1,0:T(8,128)}) %reduce-scatter.2.cloned.1.call-update) | async-done | bytes 204816 | tf_op jit(solution)/shard_map/reduce_scatter | solution.py:204
  (266 shorter events, 45.9 us)
Async XLA Ops:
  7.2 29.5 %copy-start = (bf16[16,8,640]{2,1,0:T(8,128)(2,1)S(1)}, bf16[16,8,640]{2,1,0:T(8,128)(2,1)}, u32[]{:S(2)}) copy-start(bf16[16,8,640]{2,1,0:T(8,128)(2,1)} %param.13) | copy-start | bytes 491524
  7.2 29.5 %all-gather.3.cloned.1.call-start = ((), (), s32[]{:S(2)}) async-start(), calls=%async_computation.1 | async-start | bytes 1638400 | tf_op jit(solution)/shard_map/all_gather | solution.py:79
  9.0 231.4 %all-gather.5.cloned.1.call-start = ((), (), s32[]{:S(2)}) async-start(), calls=%async_computation.2 | async-start | bytes 6656000 | tf_op jit(solution)/shard_map/all_gather | solution.py:84
  9.8 702.0 %reduce-scatter.2.cloned.1.call-start = ((), (), s32[]{:S(2)}) async-start(), calls=%async_computation.3 | async-start | bytes 13312000 | tf_op jit(solution)/shard_map/reduce_scatter | solution.py:204
  44.7 0.9 copy-start.9
  44.7 1.0 copy-start.10
  44.7 3.0 copy-start.8
  45.7 4.4 collective-permute-start
  45.8 4.8 collective-permute-start.1
  50.6 5.5 copy-start.1
  51.5 18.9 %collective-permute-start.3 = (bf16[2,28,6,640]{3,0,2,1:T(2,128)(2,1)S(1)}, bf16[2,28,6,640]{3,0,2,1:T(2,128)(2,1)S(1)}, u32[]{:S(2)}, u32[]{:S(2)}) collective-permute-start(bf16[2,28,6,640]{3,0,2,1:T(2,128)(2,1)S(1)} %copy.59), channel_id=1, source_target_pairs={{4,0},{8,4},{12,8},{16,12},{20,16},{24,20},{28,24},{0,28},{5,1},{9... | collective-permute-start | bytes 1290248 | tf_op jit(solution)/shard_map/ppermute | solution.py:18
  56.1 24.8 %collective-permute-start.2 = (bf16[2,28,6,640]{3,0,2,1:T(2,128)(2,1)S(1)}, bf16[2,28,6,640]{3,0,2,1:T(2,128)(2,1)S(1)}, u32[]{:S(2)}, u32[]{:S(2)}) collective-permute-start(bf16[2,28,6,640]{3,0,2,1:T(2,128)(2,1)S(1)} %copy.58), channel_id=1, source_target_pairs={{0,4},{4,8},{8,12},{12,16},{16,20},{20,24},{24,28},{28,0},{1,5},{5... | collective-permute-start | bytes 1290248 | tf_op jit(solution)/shard_map/ppermute | solution.py:17
  81.0 159.4 %copy-start.11 = (bf16[16,8,5120]{2,0,1:T(8,128)(2,1)S(1)}, bf16[16,8,5120]{2,0,1:T(8,128)(2,1)}, u32[]{:S(2)}) copy-start(bf16[16,8,5120]{2,0,1:T(8,128)(2,1)} %all-gather.3.cloned.1.call-done) | copy-start | bytes 3932164
  246.9 13.4 %copy-start.12 = (bf16[16,8,5,128]{3,1,2,0:T(8,128)(2,1)}, bf16[16,8,5,128]{3,1,2,0:T(8,128)(2,1)S(1)}, u32[]{:S(2)}) copy-start(bf16[16,8,5,128]{3,1,2,0:T(8,128)(2,1)S(1)} %get-tuple-element.541) | copy-start | bytes 491524 | tf_op jit(solution)/shard_map/while
  271.5 1.5 copy-start.2
  271.9 1.3 copy-start.3
  273.2 3.1 copy-start.13
  276.2 13.4 %copy-start.12 = (bf16[16,8,5,128]{3,1,2,0:T(8,128)(2,1)}, bf16[16,8,5,128]{3,1,2,0:T(8,128)(2,1)S(1)}, u32[]{:S(2)}) copy-start(bf16[16,8,5,128]{3,1,2,0:T(8,128)(2,1)S(1)} %get-tuple-element.541) | copy-start | bytes 491524 | tf_op jit(solution)/shard_map/while
  300.8 1.5 copy-start.2
  301.2 1.3 copy-start.3
  302.4 3.1 copy-start.13
  305.5 13.4 %copy-start.12 = (bf16[16,8,5,128]{3,1,2,0:T(8,128)(2,1)}, bf16[16,8,5,128]{3,1,2,0:T(8,128)(2,1)S(1)}, u32[]{:S(2)}) copy-start(bf16[16,8,5,128]{3,1,2,0:T(8,128)(2,1)S(1)} %get-tuple-element.541) | copy-start | bytes 491524 | tf_op jit(solution)/shard_map/while
  330.1 1.5 copy-start.2
  330.5 1.3 copy-start.3
  331.7 3.1 copy-start.13
  334.8 13.4 %copy-start.12 = (bf16[16,8,5,128]{3,1,2,0:T(8,128)(2,1)}, bf16[16,8,5,128]{3,1,2,0:T(8,128)(2,1)S(1)}, u32[]{:S(2)}) copy-start(bf16[16,8,5,128]{3,1,2,0:T(8,128)(2,1)S(1)} %get-tuple-element.541) | copy-start | bytes 491524 | tf_op jit(solution)/shard_map/while
  359.4 1.5 copy-start.2
  359.8 1.3 copy-start.3
  361.1 3.1 copy-start.13
  366.5 4.3 copy-start.4
  366.5 4.3 copy-start.6
  366.5 4.7 copy-start.14
  368.8 159.4 %collective-permute-start.5 = (bf16[2,28,6,640]{3,0,2,1:T(2,128)(2,1)}, bf16[2,28,6,640]{3,0,2,1:T(2,128)(2,1)}, u32[]{:S(2)}, u32[]{:S(2)}) collective-permute-start(bf16[2,28,6,640]{3,0,2,1:T(2,128)(2,1)} %copy.71), channel_id=1, source_target_pairs={{4,0},{8,4},{12,8},{16,12},{20,16},{24,20},{28,24},{0,28},{5,1},{9... | collective-permute-start | bytes 1290248 | tf_op jit(solution)/shard_map/ppermute | solution.py:18
  368.8 160.5 %collective-permute-start.4 = (bf16[2,28,6,640]{3,0,2,1:T(2,128)(2,1)}, bf16[2,28,6,640]{3,0,2,1:T(2,128)(2,1)}, u32[]{:S(2)}, u32[]{:S(2)}) collective-permute-start(bf16[2,28,6,640]{3,0,2,1:T(2,128)(2,1)} %copy.70), channel_id=1, source_target_pairs={{0,4},{4,8},{8,12},{12,16},{16,20},{20,24},{24,28},{28,0},{1,5},{5... | collective-permute-start | bytes 1290248 | tf_op jit(solution)/shard_map/ppermute | solution.py:17
  370.8 1.7 copy-start.19
  370.8 1.7 copy-start.15
  370.8 1.7 copy-start.17
  527.8 2.6 copy-start.5
  527.8 2.6 copy-start.7
  530.4 0.7 copy-start.21
  531.1 8.0 %copy-start.16 = (s32[8,13]{1,0:T(8,128)S(1)}, s32[8,13]{1,0:T(8,128)}, u32[]{:S(2)}) copy-start(s32[8,13]{1,0:T(8,128)} %copy-done.15) | copy-start | bytes 1252
  531.1 8.0 %copy-start.18 = (s32[8,13]{1,0:T(8,128)S(1)}, s32[8,13]{1,0:T(8,128)}, u32[]{:S(2)}) copy-start(s32[8,13]{1,0:T(8,128)} %copy-done.17) | copy-start | bytes 1252
  531.1 8.1 %copy-start.20 = (pred[8,13]{1,0:T(8,128)(4,1)S(1)}, pred[8,13]{1,0:T(8,128)(4,1)}, u32[]{:S(2)}) copy-start(pred[8,13]{1,0:T(8,128)(4,1)} %copy-done.19) | copy-start | bytes 316
  533.5 97.7 %copy-start.22 = (pred[16]{0:T(512)(128)(4,1)S(1)}, pred[16]{0:T(512)(128)(4,1)}, u32[]{:S(2)}) copy-start(pred[16]{0:T(512)(128)(4,1)} %constant.227.clone.1) | copy-start | bytes 52
  533.5 97.6 %collective-permute-start.6 = (bf16[2,6,8,640]{3,2,1,0:T(8,128)(2,1)S(1)}, bf16[2,6,8,640]{3,2,1,0:T(8,128)(2,1)S(1)}, u32[]{:S(2)}, u32[]{:S(2)}) collective-permute-start(bf16[2,6,8,640]{3,2,1,0:T(8,128)(2,1)S(1)} %get-tuple-element.361), channel_id=1, source_target_pairs={{0,32},{32,64},{64,96},{96,128},{128,160},{160,192},{192,224},{1,3... | collective-permute-start | bytes 368648 | tf_op jit(solution)/shard_map/ppermute | solution.py:17
  535.4 95.7 %collective-permute-start.7 = (bf16[2,6,8,640]{3,2,1,0:T(8,128)(2,1)S(1)}, bf16[2,6,8,640]{3,2,1,0:T(8,128)(2,1)S(1)}, u32[]{:S(2)}, u32[]{:S(2)}) collective-permute-start(bf16[2,6,8,640]{3,2,1,0:T(8,128)(2,1)S(1)} %get-tuple-element.362), channel_id=1, source_target_pairs={{32,0},{64,32},{96,64},{128,96},{160,128},{192,160},{224,192},{33,... | collective-permute-start | bytes 368648 | tf_op jit(solution)/shard_map/ppermute | solution.py:18
Sparse Core Ops, SparseCore 0:
  9.8 26.8 all-gather.2
  38.5 201.8 all-gather.4
  243.5 468.2 reduce-scatter.1
